TPU v7x, 768 devices: a whole 4x8x12 slice. The times are simulated.
768 devices in a mesh: ctx: 64 (over x, y, core), tp: 12 (over z).
Axes of the slice: x: 4, y: 8, z: 12, core: 2. Of those that a mesh axis runs over, the one named last changes fastest.
Arguments:
- tokens: bfloat16 [16384, 2048], P('ctx'), may hold values from -12 to 12
- feature_weight: bfloat16 [2048, 384], P(None, 'tp'), may hold values from -0.125 to 0.125
- window_weight: bfloat16 [2048, 3072], P(None, 'tp'), may hold values from -1 to 1
- value_weight: bfloat16 [2048, 1536], P(None, 'tp'), may hold values from -0.125 to 0.125
- log_decay: float32 [16384, 12], P('ctx', 'tp'), may hold values from -1 to 0
- out_grad: bfloat16 [16384, 1536], P('ctx', 'tp'), may hold values from -6 to 6
Outputs:
- attended: bfloat16 [16384, 1536], P('ctx', 'tp')
- input_grad: bfloat16 [16384, 2048], P('ctx')
All inputs are finite; a program needn't handle non-finite values.
Results may differ from a plain program's by a relative error of at most 0.012.
The roundings to bfloat16 on the way count: a program that leaves them out, or rounds other values in their place, can miss the bound.
Values may be sent and summed in bfloat16 or wider, within the bound.
A program may use at most 64 MiB of HBM per device.

v0:
```python
from functools import partial

import jax
import jax.numpy as jnp
from jax import lax
from jax.sharding import PartitionSpec as P

WINDOW = 1024


precise = lax.Precision.HIGHEST


def carried_in(part, axis, combine, identity):
    place = lax.axis_index(axis)
    gathered = jax.tree.map(lambda a: lax.all_gather(a, axis), part)
    state = jax.tree.map(lambda a, e: jnp.zeros_like(a) + jnp.asarray(e, a.dtype), part, identity)

    def one(step, state):
        return combine(
            state, jax.tree.map(lambda a: lax.dynamic_index_in_dim(a, step, 0, False), gathered)
        )

    return lax.fori_loop(0, place, one, state)


def shifted(value, axis, by):
    count = lax.axis_size(axis)
    pairs = [(i, i + by) for i in range(count) if 0 <= i + by < count]
    return lax.ppermute(value, axis, pairs)


def entering(value, axis, combine, identity):
    count, mine = (lax.axis_size(axis), lax.axis_index(axis))
    everything = jax.tree.map(
        lambda part, kind: lax.all_gather(part.astype(kind), axis),
        value,
        jax.tree.map(lambda a: jnp.bfloat16 if a.dtype == jnp.float32 else a.dtype, value),
    )
    start = jax.tree.map(
        lambda part, zero: jnp.broadcast_to(jnp.asarray(zero, part.dtype), part.shape),
        value,
        identity,
    )

    def step(k, before):
        at = count - 1 - k
        reached = at > mine
        new = combine(
            before, jax.tree.map(lambda part, own: part[at].astype(own.dtype), everything, value)
        )
        return jax.tree.map(lambda a, b: jnp.where(reached, a, b), new, before)

    return lax.fori_loop(0, count, step, start)


def feature_map(vectors):
    row_count = vectors.shape[0]
    feat_width = vectors.shape[1]
    square = (vectors[:, :, None] * vectors[:, None, :]).reshape(
        row_count, feat_width * feat_width
    ) * 0.5**0.5
    return jnp.concatenate([square, vectors, jnp.ones((row_count, 1), jnp.float32)], axis=1)


def linear_part(
    query_feat, query_cum, query_pos, key_feat, key_cum, key_pos, value_rows, state_num, state_den
):
    products = jnp.dot(query_feat, key_feat.T, precision=precise)
    kernel = 1.0 + products + 0.5 * products * products
    causal = key_pos[None, :] <= query_pos[:, None]
    decay_table = jnp.exp(jnp.where(causal, query_cum[:, None] - key_cum[None, :], -jnp.inf))
    weights = kernel * decay_table
    lifted = feature_map(query_feat)
    growth = jnp.exp(query_cum)
    numerator = jnp.dot(weights, value_rows, precision=precise) + growth[:, None] * jnp.dot(
        lifted, state_num, precision=precise
    )
    denominator = jnp.sum(weights, axis=1) + growth * jnp.dot(lifted, state_den, precision=precise)
    return numerator / denominator[:, None]


def window_part(queries, query_pos, key_rows, key_values, key_pos):
    head_dim = queries.shape[1]
    scores = jnp.dot(queries, key_rows.T, precision=precise) * head_dim ** (-0.5)
    allowed = (
        (key_pos[None, :] <= query_pos[:, None])
        & (query_pos[:, None] - key_pos[None, :] < WINDOW)
        & (key_pos[None, :] >= 0)
    )
    scores = jnp.where(allowed, scores, -jnp.inf)
    row_max = jnp.max(scores, axis=1, keepdims=True)
    exponent = jnp.exp(scores - row_max)
    return jnp.dot(exponent, key_values, precision=precise) / jnp.sum(
        exponent, axis=1, keepdims=True
    )


def combine_states(earlier, later):
    factor = jnp.exp(later[0])
    return (earlier[0] + later[0], factor * earlier[1] + later[1], factor * earlier[2] + later[2])


def local_state(feat_cols, val_cols, cumulative):
    feat_dim = feat_cols.shape[1] // 2
    key_feat = feat_cols[:, feat_dim:] * feat_dim ** (-0.25)
    tail_decay = jnp.exp(cumulative[-1] - cumulative)
    phi_keys = feature_map(key_feat) * tail_decay[:, None]
    return (jnp.dot(phi_keys.T, val_cols, precision=precise), jnp.sum(phi_keys, axis=0))


def local_output(
    feat_cols, win_cols, val_cols, halo_rows, state_num, state_den, cumulative, first_pos
):
    rows_here = feat_cols.shape[0]
    feat_dim = feat_cols.shape[1] // 2
    head_dim = val_cols.shape[1]
    feat_scale = feat_dim ** (-0.25)
    query_feat = feat_cols[:, :feat_dim] * feat_scale
    key_feat = feat_cols[:, feat_dim:] * feat_scale
    queries = win_cols[:, :head_dim]
    all_keys = jnp.concatenate([halo_rows[:, :head_dim], win_cols[:, head_dim:]], axis=0)
    all_values = jnp.concatenate([halo_rows[:, head_dim:], val_cols], axis=0)
    halo_span = halo_rows.shape[0]
    local_pos = jnp.arange(rows_here, dtype=jnp.int32)
    block_rows = min(rows_here, 512)
    linear = linear_part(
        query_feat,
        cumulative,
        local_pos,
        key_feat,
        cumulative,
        local_pos,
        val_cols,
        state_num,
        state_den,
    )
    key_pos = 0 - halo_span + jnp.arange(block_rows + halo_span, dtype=jnp.int32)
    windowed = window_part(
        queries, first_pos + local_pos, all_keys, all_values, first_pos + key_pos
    )
    pieces = [linear + windowed]
    return jnp.concatenate(pieces, axis=0)


def head_terms(grad_rows, feature_weight, window_weight, value_weight):
    return (
        jnp.dot(grad_rows[0], feature_weight.T, preferred_element_type=jnp.float32)
        + jnp.dot(grad_rows[1], window_weight.T, preferred_element_type=jnp.float32)
        + jnp.dot(grad_rows[2], value_weight.T, preferred_element_type=jnp.float32)
    )


def per_device(tokens, feature_weight, window_weight, value_weight, log_decay, out_grad):
    rows_here = tokens.shape[0]
    head_dim = value_weight.shape[1]
    features = jnp.dot(tokens, feature_weight, preferred_element_type=jnp.float32).astype(
        jnp.bfloat16
    )
    window = jnp.dot(tokens, window_weight, preferred_element_type=jnp.float32).astype(jnp.bfloat16)
    values = jnp.dot(tokens, value_weight, preferred_element_type=jnp.float32).astype(jnp.bfloat16)
    cumulative = jnp.cumsum(log_decay[:, 0])
    feat_cols = features.astype(jnp.float32)
    win_cols = window.astype(jnp.float32)
    val_cols = values.astype(jnp.float32)
    state_num, state_den = local_state(feat_cols, val_cols, cumulative)
    decay_total = cumulative[-1:]
    identity = (jnp.zeros((1,), jnp.float32), jnp.zeros_like(state_num), jnp.zeros_like(state_den))
    incoming = carried_in((decay_total, state_num, state_den), "ctx", combine_states, identity)
    pair_rows = jnp.concatenate([window[:, head_dim:], values], axis=1)
    blocks_back = WINDOW // rows_here
    fetched = [shifted(pair_rows, "ctx", distance) for distance in range(blocks_back, 0, -1)]
    halo_rows = jnp.concatenate(fetched, axis=0)
    first_pos = lax.axis_index("ctx") * rows_here
    output_fn = partial(local_output, cumulative=cumulative, first_pos=first_pos)
    result, pullback = jax.vjp(
        output_fn,
        feat_cols,
        win_cols,
        val_cols,
        halo_rows.astype(jnp.float32),
        incoming[1],
        incoming[2],
    )
    attended = result.astype(jnp.bfloat16)
    grad_feat, grad_win, grad_val, grad_halo, grad_num, grad_den = pullback(
        out_grad.astype(jnp.float32)
    )
    outgoing = entering((decay_total, grad_num, grad_den), "ctx", combine_states, identity)
    state_pull = jax.vjp(partial(local_state, cumulative=cumulative), feat_cols, val_cols)[1]
    more_feat, more_val = state_pull((outgoing[1], outgoing[2]))
    returned = jnp.zeros((rows_here, 2 * head_dim), jnp.float32)
    for distance in range(1, blocks_back + 1):
        offset = (blocks_back - distance) * rows_here
        returned = returned + shifted(grad_halo[offset : offset + rows_here], "ctx", -distance)
    grad_win = jnp.concatenate(
        [grad_win[:, :head_dim], grad_win[:, head_dim:] + returned[:, :head_dim]], axis=1
    )
    grad_val = grad_val + more_val + returned[:, head_dim:]
    grad_feat = grad_feat + more_feat
    grad_rows = (
        grad_feat.astype(jnp.bfloat16),
        grad_win.astype(jnp.bfloat16),
        grad_val.astype(jnp.bfloat16),
    )
    partial_sum = head_terms(grad_rows, feature_weight, window_weight, value_weight)
    input_grad = lax.psum(partial_sum, "tp").astype(jnp.bfloat16)
    return (attended, input_grad)


def solution(mesh):
    in_specs = (
        P("ctx", None),
        P(None, "tp"),
        P(None, "tp"),
        P(None, "tp"),
        P("ctx", "tp"),
        P("ctx", "tp"),
    )
    out_specs = (P("ctx", "tp"), P("ctx", None))
    return jax.shard_map(
        per_device, mesh=mesh, in_specs=in_specs, out_specs=out_specs, check_vma=False
    )
```

profile of v0, /device:TPU:64, one launch (start us, length us, event | category | flops | bytes accessed | tf_op | source)
XLA Modules:
  0.0 1120.7 jit_solution(16984072643862229539)
XLA Ops:
  11.8 1.6 fusion.9
  17.7 129.2 %all-reduce.7 = f32[64]{0:T(128)S(1)} all-reduce(f32[64]{0:T(128)S(1)} %get-tuple-element.331), channel_id=2, replica_groups=mesh['ctx'=64,'tp'=12] {'ctx'}, use_global_device_ids=true, to_apply=%add.7 | all-reduce | flops 64 | bytes 512
  148.1 66.7 %all-reduce.15.cloned.1.call-done = f32[17472]{0:T(1024)} async-done(((f32[17472]{0:T(1024)}), f32[17472]{0:T(1024)}) %all-reduce.15.cloned.1.call-update) | async-done | bytes 69904
  215.9 94.4 %all-gather.11.cloned.1.call-done = f32[64,273,128]{2,1,0:T(8,128)} async-done(((f32[1,273,128]{2,1,0:T(8,128)}), f32[64,273,128]{2,1,0:T(8,128)}) %all-gather.11.cloned.1.call-update) | async-done | bytes 8945680 | tf_op jit(solution)/shard_map/all_gather | solution.py:16
  313.6 14.2 %collective-permute-start = (bf16[256,256]{1,0:T(8,128)(2,1)S(1)}, bf16[256,256]{1,0:T(8,128)(2,1)S(1)}, u32[]{:S(2)}, u32[]{:S(2)}) collective-permute-start(bf16[256,256]{1,0:T(8,128)(2,1)S(1)} %pad_maximum_fusion.6), channel_id=1, source_target_pairs={{0,48},{12,60},{24,72},{36,84},{48,96},{60,108},{72,120},{84,132},... | collective-permute-start | bytes 393224 | tf_op jit(solution)/shard_map/ppermute | solution.py:30
  327.8 11.7 %collective-permute-start.1 = (bf16[256,256]{1,0:T(8,128)(2,1)S(1)}, bf16[256,256]{1,0:T(8,128)(2,1)S(1)}, u32[]{:S(2)}, u32[]{:S(2)}) collective-permute-start(bf16[256,256]{1,0:T(8,128)(2,1)S(1)} %pad_maximum_fusion.6), channel_id=1, source_target_pairs={{0,36},{12,48},{24,60},{36,72},{48,84},{60,96},{72,108},{84,120},{... | collective-permute-start | bytes 393224 | tf_op jit(solution)/shard_map/ppermute | solution.py:30
  339.5 8.0 collective-permute-start.2
  347.5 5.7 collective-permute-start.3
  353.3 2.0 fusion.73
  362.3 2.3 fusion.31
  364.6 1.6 fusion.84
  380.1 400.7 %all-reduce.11 = (bf16[64]{0:T(256)(128)(2,1)}, bf16[17472]{0:T(1024)(128)(2,1)S(1)}) all-reduce(bf16[64]{0:T(256)(128)(2,1)} %copy-done.50, bf16[17472]{0:T(1024)(128)(2,1)S(1)} %dynamic-update-slice.3), channel_id=5, replica_groups=mesh['ctx'=64,'tp'=12] {'ctx'}, use_global_device_ids=true, to_apply=%add.9 | all-reduce | flops 17536 | bytes 70144
  781.5 1.6 copy.24
  783.1 3.0 fusion.14
  788.9 260.2 %while.33 = (s32[]{:T(128)}, f32[273,128]{1,0:T(8,128)S(1)}, f32[273]{0:T(512)S(1)}, s32[]{:T(128)}, bf16[64,1]{0,1:T(2,128)(2,1)}, /*index=5*/bf16[64,273,128]{...) while((s32[]{:T(128)}, f32[273,128]{1,0:T(8,128)S(1)}, ...), condition=%wide.region_12.13_spmd.clone, body=%wide.region_11.12_spmd.clone.sunk | while | flops 176093 | bytes 354557 | solution.py:54
  814.5 1.5 fusion.111
  822.6 1.5 fusion.111
  830.7 1.5 fusion.111
  838.9 1.5 fusion.111
  847.0 1.5 fusion.111
  855.1 1.5 fusion.111
  875.5 1.5 fusion.111
  879.6 1.5 fusion.111
  891.8 1.5 fusion.111
  899.9 1.5 fusion.111
  908.0 1.5 fusion.111
  916.2 1.5 fusion.111
  924.3 1.5 fusion.111
  960.9 1.5 fusion.111
  969.0 1.5 fusion.111
  1049.1 1.6 convolution_add_fusion.6
  1053.6 60.6 %all-reduce.16 = bf16[256,2048]{1,0:T(8,128)(2,1)} all-reduce(f32[256,2048]{1,0:T(8,128)S(1)} %convolution_add_fusion.2), channel_id=1, replica_groups=mesh['ctx'=64,'tp'=12] {'tp'}, use_global_device_ids=true, to_apply=%region_18.19 | all-reduce | flops 524288 | bytes 3145728 | tf_op jit(solution)/shard_map/psum | solution.py:207
  (444 shorter events, 276.2 us)
Async XLA Ops:
  7.2 305.2 %copy-start = (bf16[2048,256]{1,0:T(8,128)(2,1)S(1)}, bf16[2048,256]{1,0:T(8,128)(2,1)}, u32[]{:S(2)}) copy-start(bf16[2048,256]{1,0:T(8,128)(2,1)} %param.12) | copy-start | bytes 3145732
  7.2 8.2 copy-start.1
  7.2 8.2 copy-start.4
  7.2 207.6 %all-reduce.15.cloned.1.call-start = ((), (), s32[]{:S(2)}) async-start(), calls=%async_computation | async-start | bytes 147456
  8.7 302.0 %copy-start.38 = (f32[256]{0:T(256)}, f32[256]{0:T(256)S(1)}, u32[]{:S(2)}) copy-start(f32[256]{0:T(256)S(1)} %get-tuple-element.313) | copy-start | bytes 3076
  8.7 302.6 %copy-start.42 = (f32[256]{0:T(256)}, f32[256]{0:T(256)S(1)}, u32[]{:S(2)}) copy-start(f32[256]{0:T(256)S(1)} %get-tuple-element.312) | copy-start | bytes 3076
  13.4 133.5 %copy-start.27 = (f32[256,32]{0,1:T(8,128)}, f32[256,32]{0,1:T(8,128)S(1)}, u32[]{:S(2)}) copy-start(f32[256,32]{0,1:T(8,128)S(1)} %fusion.9) | copy-start | bytes 98308
  13.5 297.8 %copy-start.18 = (f32[256,16]{0,1:T(8,128)}, f32[256,16]{0,1:T(8,128)S(1)}, u32[]{:S(2)}) copy-start(f32[256,16]{0,1:T(8,128)S(1)} %get-tuple-element.326) | copy-start | bytes 49156
  14.2 297.1 %copy-start.35 = (f32[273]{0:T(512)}, f32[273]{0:T(512)S(1)}, u32[]{:S(2)}) copy-start(f32[273]{0:T(512)S(1)} %pad.45.clone) | copy-start | bytes 3280
  15.4 295.0 %all-gather.11.cloned.1.call-start = ((), (), s32[]{:S(2)}) async-start(), calls=%async_computation.1 | async-start | bytes 9318400 | tf_op jit(solution)/shard_map/all_gather | solution.py:16
  16.5 359.3 %copy-start.8 = (bf16[256,128]{1,0:T(8,128)(2,1)}, bf16[256,128]{1,0:T(8,128)(2,1)S(1)}, u32[]{:S(2)}) copy-start(bf16[256,128]{1,0:T(8,128)(2,1)S(1)} %get-tuple-element.337) | copy-start | bytes 196612
  17.5 771.2 %all-gather.13.cloned.1.call-start = ((), (), s32[]{:S(2)}) async-start(), calls=%async_computation.2 | async-start | bytes 4659200 | tf_op jit(solution)/shard_map/all_gather | solution.py:36
  17.7 293.6 %copy-start.16 = (bf16[256,128]{0,1:T(8,128)(2,1)}, bf16[256,128]{0,1:T(8,128)(2,1)S(1)}, u32[]{:S(2)}) copy-start(bf16[256,128]{0,1:T(8,128)(2,1)S(1)} %copy.18) | copy-start | bytes 196612
  146.9 164.4 %copy-start.13 = (f32[256,16,16]{0,2,1:T(8,128)}, f32[256,16,16]{0,2,1:T(8,128)S(1)}, u32[]{:S(2)}) copy-start(f32[256,16,16]{0,2,1:T(8,128)S(1)} %multiply_multiply_fusion.2) | copy-start | bytes 786436
  312.4 40.9 %copy-start.39 = (f32[256]{0:T(256)S(1)}, f32[256]{0:T(256)}, u32[]{:S(2)}) copy-start(f32[256]{0:T(256)} %copy-done.38) | copy-start | bytes 3076
  312.9 44.9 %copy-start.24 = (bf16[256,256]{1,0:T(8,128)(2,1)}, bf16[256,256]{1,0:T(8,128)(2,1)S(1)}, u32[]{:S(2)}) copy-start(bf16[256,256]{1,0:T(8,128)(2,1)S(1)} %convolution_convert_fusion) | copy-start | bytes 393220
  313.6 43.6 %collective-permute-start = (bf16[256,256]{1,0:T(8,128)(2,1)S(1)}, bf16[256,256]{1,0:T(8,128)(2,1)S(1)}, u32[]{:S(2)}, u32[]{:S(2)}) collective-permute-start(bf16[256,256]{1,0:T(8,128)(2,1)S(1)} %pad_maximum_fusion.6), channel_id=1, source_target_pairs={{0,48},{12,60},{24,72},{36,84},{48,96},{60,108},{72,120},{84,132},... | collective-permute-start | bytes 393224 | tf_op jit(solution)/shard_map/ppermute | solution.py:30
  327.8 29.4 %collective-permute-start.1 = (bf16[256,256]{1,0:T(8,128)(2,1)S(1)}, bf16[256,256]{1,0:T(8,128)(2,1)S(1)}, u32[]{:S(2)}, u32[]{:S(2)}) collective-permute-start(bf16[256,256]{1,0:T(8,128)(2,1)S(1)} %pad_maximum_fusion.6), channel_id=1, source_target_pairs={{0,36},{12,48},{24,60},{36,72},{48,84},{60,96},{72,108},{84,120},{... | collective-permute-start | bytes 393224 | tf_op jit(solution)/shard_map/ppermute | solution.py:30
  339.5 17.7 %collective-permute-start.2 = (bf16[256,256]{1,0:T(8,128)(2,1)S(1)}, bf16[256,256]{1,0:T(8,128)(2,1)S(1)}, u32[]{:S(2)}, u32[]{:S(2)}) collective-permute-start(bf16[256,256]{1,0:T(8,128)(2,1)S(1)} %pad_maximum_fusion.6), channel_id=1, source_target_pairs={{0,24},{12,36},{24,48},{36,60},{48,72},{60,84},{72,96},{84,108},{9... | collective-permute-start | bytes 393224 | tf_op jit(solution)/shard_map/ppermute | solution.py:30
  347.5 9.8 collective-permute-start.3
  353.3 13.0 %copy-start.44 = (pred[1280]{0:T(1024)(128)(4,1)}, pred[1280]{0:T(1024)(128)(4,1)S(1)}, u32[]{:S(2)}) copy-start(pred[1280]{0:T(1024)(128)(4,1)S(1)} %broadcast_compare_fusion.1) | copy-start | bytes 3844
  357.2 9.0 copy-start.41
  359.9 6.3 copy-start.23
  367.5 12.3 %copy-start.15 = (f32[1280,128]{0,1:T(8,128)}, f32[1280,128]{0,1:T(8,128)S(1)}, u32[]{:S(2)}) copy-start(f32[1280,128]{0,1:T(8,128)S(1)} %fusion.15) | copy-start | bytes 1966084
  369.9 5.9 copy-start.40
  369.9 5.9 copy-start.53
  369.9 416.2 %collective-permute-start.4 = (f32[256,256]{0,1:T(8,128)}, f32[256,256]{0,1:T(8,128)}, u32[]{:S(2)}, u32[]{:S(2)}) collective-permute-start(f32[256,256]{0,1:T(8,128)} %get-tuple-element.316), channel_id=1, source_target_pairs={{12,0},{24,12},{36,24},{48,36},{60,48},{72,60},{84,72},{96,84},{10... | collective-permute-start | bytes 786440 | tf_op jit(solution)/shard_map/ppermute | solution.py:30
  371.3 414.8 %collective-permute-start.5 = (f32[256,256]{0,1:T(8,128)}, f32[256,256]{0,1:T(8,128)}, u32[]{:S(2)}, u32[]{:S(2)}) collective-permute-start(f32[256,256]{0,1:T(8,128)} %get-tuple-element.315), channel_id=1, source_target_pairs={{24,0},{36,12},{48,24},{60,36},{72,48},{84,60},{96,72},{108,84},{1... | collective-permute-start | bytes 786440 | tf_op jit(solution)/shard_map/ppermute | solution.py:30
  372.6 413.5 %collective-permute-start.6 = (f32[256,256]{0,1:T(8,128)}, f32[256,256]{0,1:T(8,128)}, u32[]{:S(2)}, u32[]{:S(2)}) collective-permute-start(f32[256,256]{0,1:T(8,128)} %get-tuple-element.318), channel_id=1, source_target_pairs={{36,0},{48,12},{60,24},{72,36},{84,48},{96,60},{108,72},{120,84},{... | collective-permute-start | bytes 786440 | tf_op jit(solution)/shard_map/ppermute | solution.py:30
  373.9 412.2 %collective-permute-start.7 = (f32[256,256]{0,1:T(8,128)}, f32[256,256]{0,1:T(8,128)}, u32[]{:S(2)}, u32[]{:S(2)}) collective-permute-start(f32[256,256]{0,1:T(8,128)} %get-tuple-element.317), channel_id=1, source_target_pairs={{48,0},{60,12},{72,24},{84,36},{96,48},{108,60},{120,72},{132,84},... | collective-permute-start | bytes 786440 | tf_op jit(solution)/shard_map/ppermute | solution.py:30
  376.4 406.7 %copy-start.7 = (f32[256,1280]{1,0:T(8,128)S(1)}, f32[256,1280]{1,0:T(8,128)}, u32[]{:S(2)}) copy-start(f32[256,1280]{1,0:T(8,128)} %copy-done.6) | copy-start | bytes 3932164
  376.4 406.7 %copy-start.45 = (pred[1280]{0:T(1024)(128)(4,1)S(1)}, pred[1280]{0:T(1024)(128)(4,1)}, u32[]{:S(2)}) copy-start(pred[1280]{0:T(1024)(128)(4,1)} %copy-done.44) | copy-start | bytes 3844
  (35 other events, 59.1 us)
Sparse Core Ops, SparseCore 0:
  15.5 199.3 all-reduce.14
  218.7 91.6 all-gather.10
  314.3 256.2 all-gather.12
where the time goes:
time: 1130 us; the launch traced here: 1120 us
  blocking collectives  590 us (52%)
  other arithmetic  186 us (16%)
  waiting for transfers between devices  161 us (14%)
  local copies, waits for them, and re-layouts  93.5 us (8%)
  starting transfers between devices  45 us (4%)
  matrix products  27.6 us (2%)
  between operations  15.3 us (1%)
    unnamed x2, blocking collectives  530 us
    select_n x128, other arithmetic, step(): return jax.tree.map(lambda a, b: jnp.where(reached, a, b), new, before)  133 us
    all_gather x1, waiting for transfers between devices, carried_in(): gathered = jax.tree.map(lambda a: lax.all_gather(a, axis), part)  94.4 us
    exp x64, local copies, waits for them, and re-layouts, combine_states(): factor = jnp.exp(later[0])  79.5 us
    unnamed x4, waiting for transfers between devices  66.8 us
    psum x1, blocking collectives, per_device(): input_grad = lax.psum(partial_sum, 'tp').astype(jnp.bfloat16)  60.6 us
    convert_element_type x64, other arithmetic, step(): part[at].astype(own.dtype)  46 us
    ppermute x8, starting transfers between devices, shifted(): return lax.ppermute(value, axis, pairs)  44.9 us
  transfers between devices with their start and end apart: 11, of which 2 were waited for; matrix products, arithmetic and copies ran while one was open for 3% of the time, Pallas kernels for 0%

commit v1 on v0

v1 whole, which is shorter than its diff:
```python
import jax
import jax.numpy as jnp
from jax import lax
from jax.experimental import pallas as pl
from jax.experimental.pallas import tpu as pltpu
from jax.sharding import PartitionSpec as P

F32 = jnp.float32
BF = jnp.bfloat16
MESH = pl.DeviceIdType.MESH
ROWS = 256
DH = 128
D = 2048
FEATS = 256
HALF = 96
SHARD = 352
SUB = 176
NEG = -1e30


def dot(a, b, ca, cb, precision=None):
    return lax.dot_general(
        a, b, (((ca,), (cb,)), ((), ())), precision=precision, preferred_element_type=F32
    )


def nn(a, b):
    return dot(a, b, 1, 0)


def nt(a, b):
    return dot(a, b, 1, 1)


def tn(a, b):
    return dot(a, b, 0, 0)


def iota(shape, dim):
    return lax.broadcasted_iota(jnp.int32, shape, dim)


def selections(offset):
    row = iota((32, FEATS), 0) - offset
    f = iota((32, FEATS), 1)
    low = f & 15
    pair = f < 136
    linear = (f >= 144) & (f < 160)
    first = (row == low) & (pair | linear)
    second = (row == ((low + (f >> 4)) & 15)) & pair
    return (
        jnp.where(first, 1.0, 0.0).astype(BF),
        jnp.where(second, 1.0, 0.0).astype(BF),
    )


def rate_of(block):
    return block[84:85] + block[85:86]


def with_rate(block, rate):
    row = iota((HALF, DH), 0)
    high = rate.astype(BF).astype(F32)
    return jnp.where(row == 84, high, jnp.where(row == 85, rate - high, block)).astype(BF)


def kernel_body(ctx_n, tp_n):
    ynum, xnum = 8, ctx_n // 16
    links = tp_n // 2
    back = tp_n - 1 - links

    def body(
        tok_h, wf_h, ww_h, wv_h, ld_ref, og_ref,
        att_ref, ig_ref,
        tok, wf, ww, wv, insem,
        kv, kvs, kvr,
        msg, pm, hb, yb, rb, xb, pb, po,
        cs, cr, ys, yr, xs, xr,
        dkv0, dkv2, dkv4, dsend, prt, m2, m1, r2, r1, gs, gr,
        part, res, rsb, rss, rsr, ags, agr,
    ):
        i = lax.axis_index("ctx")
        z = lax.axis_index("tp")
        c = lax.rem(i, 2)
        chip = i // 2
        y = lax.rem(chip, ynum)
        x = chip // ynum
        partner = i + 1 - 2 * c
        after = lax.rem(i + 2, ctx_n)
        before = lax.rem(i + ctx_n - 2, ctx_n)
        up = lax.rem(z + 1, tp_n)
        down = lax.rem(z + tp_n - 1, tp_n)

        def y_peer(k):
            return (x * ynum + lax.rem(y + k + ynum, ynum)) * 2 + c

        def x_peer(k):
            return (lax.rem(x + k + xnum, xnum) * ynum + y) * 2 + c

        loads = [
            pltpu.make_async_copy(a, b, insem.at[n])
            for n, (a, b) in enumerate(((tok_h, tok), (wf_h, wf), (wv_h, wv), (ww_h, ww)))
        ]
        for one in loads:
            one.start()
        barrier = pltpu.get_barrier_semaphore()
        peers = [{"ctx": partner}, {"ctx": after}, {"ctx": before}, {"tp": up}, {"tp": down}]
        peers += [{"ctx": y_peer(k)} for k in range(1, ynum)]
        peers += [{"ctx": x_peer(k)} for k in range(1, xnum)]
        for peer in peers:
            pl.semaphore_signal(barrier, inc=1, device_id=peer, device_id_type=MESH)

        def send(src, dst, ssem, rsem, peer):
            copy = pltpu.make_async_remote_copy(
                src_ref=src, dst_ref=dst, send_sem=ssem, recv_sem=rsem,
                device_id=peer, device_id_type=MESH,
            )
            copy.start()
            return copy

        ld = jnp.broadcast_to(ld_ref[...], (DH, ROWS))
        tri = jnp.where(iota((ROWS, ROWS), 1) <= iota((ROWS, ROWS), 0), 1.0, 0.0).astype(F32)
        cum = dot(tri, ld, 1, 1, lax.Precision.HIGHEST)
        cum_row = dot(ld[0:8], tri, 1, 1, lax.Precision.HIGHEST)[0:1]
        total = cum[ROWS - 1 : ROWS]
        growth = jnp.exp(cum)
        tail = jnp.exp(total - cum)
        causal = iota((ROWS, ROWS), 1) <= iota((ROWS, ROWS), 0)
        decay = jnp.exp(jnp.where(causal, cum[:, 0:1] - cum_row, NEG))
        tail1 = tail[:, 0:1]
        growth1 = growth[:, 0:1]

        aq, bq = selections(0)
        ak, bk = selections(16)
        lane = iota((1, FEATS), 1)
        a0 = jnp.where(lane == 136, 1.0, 0.0)
        b0 = jnp.where((lane == 136) | ((lane >= 144) & (lane < 160)), 1.0, 0.0)
        wq = jnp.where(lane < 16, 0.5, 1.0)

        for n in range(3):
            loads[n].wait()
        toks = tok[...]
        fs = (nn(toks, wf[...]).astype(BF).astype(F32) * 0.5).astype(BF)
        val = nn(toks, wv[...]).astype(BF)
        og = og_ref[...]
        ka = nn(fs, ak) + a0
        kb = nn(fs, bk) + b0
        phik = ka * kb * tail1
        phik_b = phik.astype(BF)

        def message(num, den):
            row = iota((16, DH), 0)
            high = total.astype(BF).astype(F32)
            extra = jnp.where(row == 0, den[:, :DH], 0.0)
            extra = jnp.where(row == 1, den[:, DH:], extra)
            extra = jnp.where(row == 4, high, extra)
            extra = jnp.where(row == 5, total - high, extra).astype(BF)
            return jnp.concatenate(
                [num[0:80].astype(BF), extra, num[80:160].astype(BF), extra], axis=0
            )

        def scan_stages(n, cc, yy, xx, sign):
            state = {}

            def start(num, den):
                msg[n] = message(num, den)
                state["a"] = send(msg.at[n], pm.at[n], cs.at[2 * n], cr.at[2 * n], {"ctx": partner})

            def stage_y():
                state["a"].wait()
                own = msg[n, pl.ds(pl.multiple_of(c * HALF, 16), HALF)].astype(F32)
                other = pm[n, pl.ds(pl.multiple_of(c * HALF, 16), HALF)].astype(F32)
                to, tp_ = rate_of(own), rate_of(other)
                first = cc == 0
                both = jnp.where(first, jnp.exp(tp_), 1.0) * own
                both = both + jnp.where(first, 1.0, jnp.exp(to)) * other
                hb[n] = with_rate(both, to + tp_)
                state["y"] = [
                    send(hb.at[n], yb.at[n, k], ys.at[n, k], yr.at[n, k], {"ctx": y_peer(sign * k)})
                    for k in range(1, ynum)
                ]

            def stage_x():
                prefix = jnp.zeros((HALF, DH), F32)
                suffix = jnp.zeros((HALF, DH), F32)
                d1 = jnp.zeros((1, DH), F32)
                d2 = jnp.zeros((1, DH), F32)
                for k in range(1, ynum):
                    state["y"][k - 1].wait_recv()
                    block = yb[n, k].astype(F32)
                    rate = rate_of(block)
                    early = k <= yy
                    prefix = prefix + jnp.where(early, jnp.exp(d1), 0.0) * block
                    suffix = suffix + jnp.where(early, 0.0, jnp.exp(d2)) * block
                    d1 = d1 + jnp.where(early, rate, 0.0)
                    d2 = d2 + jnp.where(early, 0.0, rate)
                own = hb[n].astype(F32)
                rate = rate_of(own)
                row_sum = jnp.exp(d2) * (jnp.exp(rate) * prefix + own) + suffix
                rb[n] = with_rate(row_sum, d1 + rate + d2)
                state["x"] = [
                    send(rb.at[n], xb.at[n, k], xs.at[n, k], xr.at[n, k], {"ctx": x_peer(sign * k)})
                    for k in range(1, xnum)
                ]
                state["prefix"], state["d1"] = prefix, d1

            def stage_pair():
                rows = jnp.zeros((HALF, DH), F32)
                dx = jnp.zeros((1, DH), F32)
                for k in range(1, xnum):
                    state["x"][k - 1].wait_recv()
                    block = xb[n, k].astype(F32)
                    early = k <= xx
                    rows = rows + jnp.where(early, jnp.exp(dx), 0.0) * block
                    dx = dx + jnp.where(early, rate_of(block), 0.0)
                pb[n] = (state["prefix"] + jnp.exp(state["d1"]) * rows).astype(BF)
                state["b"] = send(
                    pb.at[n], po.at[n], cs.at[2 * n + 1], cr.at[2 * n + 1], {"ctx": partner}
                )

            def finish():
                state["b"].wait()
                for one in state["y"] + state["x"]:
                    one.wait_send()
                mine, theirs = pb[n].astype(F32), po[n].astype(F32)
                low = jnp.where(c == 0, mine, theirs)
                high = jnp.where(c == 0, theirs, mine)
                near = pm[n].astype(F32)
                rate = rate_of(near[0:HALF])
                second = cc == 1
                scale = jnp.where(second, jnp.exp(rate), 1.0)
                take = jnp.where(second, 1.0, 0.0)
                num = jnp.concatenate(
                    [
                        scale * low[0:80] + take * near[0:80],
                        scale * high[0:80] + take * near[96:176],
                        jnp.zeros((FEATS - 160, DH), F32),
                    ],
                    axis=0,
                ).astype(BF)
                dens = scale * low[80:82] + take * near[80:82]
                return num, jnp.concatenate([dens[0:1], dens[1:2]], axis=1)

            return start, stage_y, stage_x, stage_pair, finish

        fwd = scan_stages(0, c, y, x, 1)
        rev = scan_stages(1, 1 - c, ynum - 1 - y, xnum - 1 - x, -1)

        pl.semaphore_wait(barrier, len(peers))
        fwd[0](tn(phik_b, val), jnp.sum(phik, axis=0, keepdims=True))

        loads[3].wait()
        win = nn(toks, ww[...]).astype(BF)
        wquery = win[:, :DH]
        kv[4] = jnp.concatenate([win[:, DH:], val], axis=1)
        hop1 = send(kv.at[4], kv.at[2], kvs.at[0], kvr.at[0], {"ctx": after})

        lane32 = iota((1, 32), 1)
        perm = jnp.where(
            iota((32, 32), 0) == ((iota((32, 32), 1) + 16) & 31), 1.0, 0.0
        ).astype(BF)
        swapped = nn(fs, perm)
        fq = jnp.where(lane32 < 16, fs.astype(F32), 0.0).astype(BF)
        ks = jnp.where(lane32 < 16, swapped, 0.0).astype(BF)
        qs = jnp.where(lane32 < 16, 0.0, swapped).astype(BF)
        prod = nt(fq, ks)
        weights = (1.0 + prod + 0.5 * prod * prod) * decay
        weights_b = weights.astype(BF)
        qa = nn(fs, aq) + a0
        qb = nn(fs, bq) + b0
        phiq = qa * qb * wq
        phiq_b = phiq.astype(BF)

        fwd[1]()
        num_in = nn(weights_b, val)
        den_in = jnp.sum(weights, axis=1, keepdims=True)
        hop1.wait()
        hop2 = send(kv.at[2], kv.at[0], kvs.at[1], kvr.at[1], {"ctx": after})
        pair1 = send(kv.at[4 - 2 * c], kv.at[3], kvs.at[2], kvr.at[2], {"ctx": partner})

        fwd[2]()
        hop2.wait()
        pair2 = send(kv.at[2 - 2 * c], kv.at[1], kvs.at[3], kvr.at[3], {"ctx": partner})
        fwd[3]()
        state_num, state_den = fwd[4]()

        num = num_in + growth * nn(phiq_b, state_num)
        den = den_in + growth1 * jnp.sum(phiq * state_den, axis=1, keepdims=True)
        inv = 1.0 / den
        linear = num * inv
        ogf = og.astype(F32)
        along = jnp.sum(ogf * linear, axis=1, keepdims=True)
        dnum = ogf * inv
        gden = growth1 * (-along * inv)
        gnum = (growth * dnum).astype(BF)
        rev[0](tn(phiq_b, gnum), jnp.sum(phiq * gden, axis=0, keepdims=True))

        pair1.wait()
        pair2.wait()
        scale = DH**-0.5
        scores = []
        for d in range(5):
            s = nt(wquery, kv[4 - d, :, :DH]) * scale
            if d == 0:
                s = jnp.where(causal, s, NEG)
            elif d == 4:
                s = jnp.where(causal | (i < d), NEG, s)
            else:
                s = jnp.where(i < d, NEG, s)
            scores.append(s)
        top = jnp.max(scores[0], axis=1, keepdims=True)
        for s in scores[1:]:
            top = jnp.maximum(top, jnp.max(s, axis=1, keepdims=True))
        probs = [jnp.exp(s - top) for s in scores]
        mass = jnp.sum(probs[0], axis=1, keepdims=True)
        for p in probs[1:]:
            mass = mass + jnp.sum(p, axis=1, keepdims=True)
        imass = 1.0 / mass
        windowed = jnp.zeros((ROWS, DH), F32)
        for d in range(5):
            windowed = windowed + nn(probs[d].astype(BF), kv[4 - d, :, DH:])
        windowed = windowed * imass
        att_ref[...] = (linear + windowed).astype(BF)
        rev[1]()
        delta = jnp.sum(ogf * windowed, axis=1, keepdims=True)
        dquery = jnp.zeros((ROWS, DH), F32)
        local_dv = None
        for d in (1, 3, 4, 2, 0):
            dp = nt(og, kv[4 - d, :, DH:])
            if d == 0:
                local_dv = dp
            p = probs[d] * imass
            ds = (p * (dp - delta) * scale).astype(BF)
            dquery = dquery + nn(ds, kv[4 - d, :, :DH])
            both = jnp.concatenate([tn(ds, wquery), tn(p.astype(BF), og)], axis=1)
            if d == 1:
                dsend[0] = both.astype(BF)
            elif d == 3:
                dsend[1] = both.astype(BF)
                swap = send(dsend, prt, gs.at[0], gr.at[0], {"ctx": partner})
            else:
                {0: dkv0, 2: dkv2, 4: dkv4}[d][...] = both
        rev[2]()

        swap.wait()
        m2[...] = (dkv4[...] + jnp.where(c == 1, prt[1].astype(F32), 0.0)).astype(BF)
        ret2 = send(m2, r2, gs.at[1], gr.at[1], {"ctx": before})

        dw = (local_dv - along) * inv
        dprod = (dw * decay * (1.0 + prod)).astype(BF)
        dphiq = (nt(gnum, state_num) + gden * state_den) * wq
        dfeat = nn(dprod, ks) + tn(dprod, qs)
        dfeat = dfeat + nt((dphiq * qb).astype(BF), aq) + nt((dphiq * qa).astype(BF), bq)
        dval = tn(weights_b, dnum.astype(BF))

        rev[3]()
        ret2.wait()
        near = jnp.where(c == 0, prt[1].astype(F32), prt[0].astype(F32))
        m1[...] = (dkv2[...] + near + r2[...].astype(F32)).astype(BF)
        ret1 = send(m1, r1, gs.at[2], gr.at[2], {"ctx": before})
        back_num, back_den = rev[4]()

        dphik = tail1 * (nt(val, back_num) + back_den)
        dfeat = dfeat + nt((dphik * kb).astype(BF), ak) + nt((dphik * ka).astype(BF), bk)
        dval = dval + nn(phik_b, back_num)
        gfeat = (0.5 * dfeat).astype(BF)
        ret1.wait()
        whole = dkv0[...] + jnp.where(c == 0, prt[0].astype(F32), 0.0) + r1[...].astype(F32)
        gwin = jnp.concatenate([dquery, whole[:, :DH]], axis=1).astype(BF)
        gval = (dval + whole[:, DH:]).astype(BF)

        for j in range(D // DH):
            cut = slice(j * DH, (j + 1) * DH)
            term = nt(gwin, ww[cut]) + nt(gval, wv[cut]) + nt(gfeat, wf[cut])
            part[j * ROWS : (j + 1) * ROWS] = term.astype(BF)
        tail_rows = tp_n * SHARD - D // DH * ROWS
        part[D // DH * ROWS :] = jnp.zeros((tail_rows, DH), BF)

        def rows_of(shard, h):
            at = lax.rem(shard + 2 * tp_n, tp_n) * SHARD + h * SUB
            return pl.ds(pl.multiple_of(at, 16), SUB)

        rs = {}
        ag = {}
        for t in range(1, links + 1):
            for h in range(2):
                for way in range(2):
                    if way == 1 and t > back:
                        continue
                    shard = z + links + 1 - t if way == 0 else z - back - 1 + t
                    if t == 1:
                        src = part.at[rows_of(shard, h)]
                    else:
                        rs[way, t - 1, h].wait_recv()
                        slot = rsb.at[way, t - 1, h]
                        slot[...] = (
                            slot[...].astype(F32) + part[rows_of(shard, h)].astype(F32)
                        ).astype(BF)
                        src = slot
                    rs[way, t, h] = send(
                        src, rsb.at[way, t, h], rss.at[way, t, h], rsr.at[way, t, h],
                        {"tp": up if way == 0 else down},
                    )
        for t in range(1, links + 1):
            for h in range(2):
                if t == 1:
                    rs[0, links, h].wait_recv()
                    rs[1, back, h].wait_recv()
                    res[rows_of(z, h)] = (
                        part[rows_of(z, h)].astype(F32)
                        + rsb[0, links, h].astype(F32)
                        + rsb[1, back, h].astype(F32)
                    ).astype(BF)
                for way in range(2):
                    if way == 1 and t > back:
                        continue
                    shard = z - t + 1 if way == 0 else z + t - 1
                    if t > 1:
                        ag[way, t - 1, h].wait_recv()
                    at = rows_of(shard, h)
                    ag[way, t, h] = send(
                        res.at[at], res.at[at], ags.at[way, t, h], agr.at[way, t, h],
                        {"tp": up if way == 0 else down},
                    )
        for h in range(2):
            ag[0, links, h].wait_recv()
            ag[1, back, h].wait_recv()
        for one in list(rs.values()) + list(ag.values()):
            one.wait_send()
        for j in range(D // DH):
            ig_ref[:, j * DH : (j + 1) * DH] = res[j * ROWS : (j + 1) * ROWS]

    scratch = [
        pltpu.VMEM((ROWS, D), BF), pltpu.VMEM((D, 32), BF),
        pltpu.VMEM((D, 2 * DH), BF), pltpu.VMEM((D, DH), BF),
        pltpu.SemaphoreType.DMA((4,)),
        pltpu.VMEM((5, ROWS, 2 * DH), BF),
        pltpu.SemaphoreType.DMA((4,)), pltpu.SemaphoreType.DMA((4,)),
        pltpu.VMEM((2, 2 * HALF, DH), BF), pltpu.VMEM((2, 2 * HALF, DH), BF),
        pltpu.VMEM((2, HALF, DH), BF), pltpu.VMEM((2, 8, HALF, DH), BF),
        pltpu.VMEM((2, HALF, DH), BF), pltpu.VMEM((2, 4, HALF, DH), BF),
        pltpu.VMEM((2, HALF, DH), BF), pltpu.VMEM((2, HALF, DH), BF),
        pltpu.SemaphoreType.DMA((4,)), pltpu.SemaphoreType.DMA((4,)),
        pltpu.SemaphoreType.DMA((2, 8)), pltpu.SemaphoreType.DMA((2, 8)),
        pltpu.SemaphoreType.DMA((2, 4)), pltpu.SemaphoreType.DMA((2, 4)),
        pltpu.VMEM((ROWS, 2 * DH), F32), pltpu.VMEM((ROWS, 2 * DH), F32),
        pltpu.VMEM((ROWS, 2 * DH), F32),
        pltpu.VMEM((2, ROWS, 2 * DH), BF), pltpu.VMEM((2, ROWS, 2 * DH), BF),
        pltpu.VMEM((ROWS, 2 * DH), BF), pltpu.VMEM((ROWS, 2 * DH), BF),
        pltpu.VMEM((ROWS, 2 * DH), BF), pltpu.VMEM((ROWS, 2 * DH), BF),
        pltpu.SemaphoreType.DMA((3,)), pltpu.SemaphoreType.DMA((3,)),
        pltpu.VMEM((tp_n * SHARD, DH), BF), pltpu.VMEM((tp_n * SHARD, DH), BF),
        pltpu.VMEM((2, links + 1, 2, SUB, DH), BF),
        pltpu.SemaphoreType.DMA((2, links + 1, 2)), pltpu.SemaphoreType.DMA((2, links + 1, 2)),
        pltpu.SemaphoreType.DMA((2, links + 1, 2)), pltpu.SemaphoreType.DMA((2, links + 1, 2)),
    ]
    return body, scratch


def solution(mesh):
    ctx_n, tp_n = mesh.shape["ctx"], mesh.shape["tp"]
    body, scratch = kernel_body(ctx_n, tp_n)

    def per_device(tokens, feature_weight, window_weight, value_weight, log_decay, out_grad):
        vmem = pl.BlockSpec(memory_space=pltpu.VMEM)
        anywhere = pl.BlockSpec(memory_space=pl.ANY)
        return pl.pallas_call(
            body,
            out_shape=(
                jax.ShapeDtypeStruct((ROWS, DH), BF),
                jax.ShapeDtypeStruct((ROWS, D), BF),
            ),
            in_specs=[anywhere] * 4 + [vmem, vmem],
            out_specs=(vmem, vmem),
            scratch_shapes=scratch,
            compiler_params=pltpu.CompilerParams(
                collective_id=0, has_side_effects=True, vmem_limit_bytes=48 << 20
            ),
            name="layer",
        )(
            tokens, feature_weight, window_weight, value_weight,
            log_decay.reshape(1, ROWS), out_grad,
        )

    in_specs = (
        P("ctx", None), P(None, "tp"), P(None, "tp"), P(None, "tp"),
        P("ctx", "tp"), P("ctx", "tp"),
    )
    return jax.shard_map(
        per_device, mesh=mesh, in_specs=in_specs,
        out_specs=(P("ctx", "tp"), P("ctx", None)), check_vma=False,
    )
```

time: 1130 us -> 102 us (0.09)
  the two profiles are of different devices: /device:TPU:64 before, /device:TPU:56 now
where the time goes in v1:
time: 102 us
  Pallas kernels  96 us (94%)
  local copies, waits for them, and re-layouts  5.29 us (5%)
    pallas_call x1, Pallas kernels, per_device(): pl.pallas_call(body, out_shape=(jax.ShapeDtypeStruct((ROWS, DH), BF), jax...  96 us
    unnamed x13, local copies, waits for them, and re-layouts  5.29 us

profile of v1, /device:TPU:56, one launch (start us, length us, event | category | flops | bytes accessed | tf_op | source)
XLA Modules:
  0.0 102.0 jit_solution(15798695446005754994)
XLA Ops:
  0.6 0.0 copy-start.2
  0.6 0.0 copy-start.3
  0.7 0.0 copy-start.4
  0.7 1.2 %copy.8.wf_h = bf16[2048,32]{1,0:T(8,128)(2,1)S(1)} copy(bf16[2048,32]{0,1:T(8,128)(2,1)} %param.7) | data formatting | bytes 262144 | tf_op args[1]
  1.9 0.0 copy-done.2
  1.9 0.0 copy-done.3
  1.9 0.0 copy-done.4
  1.9 0.0 copy-start
  1.9 1.2 %copy-done = bf16[256,2048]{1,0:T(8,128)(2,1)S(1)} copy-done((bf16[256,2048]{1,0:T(8,128)(2,1)S(1)}, bf16[256,2048]{1,0:T(8,128)(2,1)}, u32[]{:S(2)}) %copy-start) | copy-done | bytes 1048600
  3.2 0.0 copy-start.1
  3.2 1.2 %copy-done.1 = bf16[2048,256]{1,0:T(8,128)(2,1)S(1)} copy-done((bf16[2048,256]{1,0:T(8,128)(2,1)S(1)}, bf16[2048,256]{1,0:T(8,128)(2,1)}, u32[]{:S(2)}) %copy-start.1) | copy-done | bytes 1048600
  4.4 96.0 %layer.1 = (bf16[256,128]{1,0:T(8,128)(2,1)S(1)}, bf16[256,2048]{1,0:T(8,128)(2,1)S(1)}) custom-call(bf16[256,2048]{1,0:T(8,128)(2,1)S(1)} %copy-done, bf16[2048,32]{1,0:T(8,128)(2,1)S(1)} %copy.8.wf_h, bf16[2048,256]{1,0:T(8,128)(2,1)S(1)} %copy-done.1, bf16[2048,128]{1,0:T(8,128)(2,1)S(1)} %copy-done.2, f32[1,256]{1,0:T(1,128)S(1)} %bitcast.1, ...), custom_call_target="tpu_custom_call" | custom-call | tf_op jit(solution)/shard_map/layer/pallas_call | solution.py:467
  100.4 0.6 copy.11
  101.0 1.0 copy.12
Async XLA Ops:
  0.6 1.3 %copy-start.2 = (bf16[2048,128]{1,0:T(8,128)(2,1)S(1)}, bf16[2048,128]{1,0:T(8,128)(2,1)}, u32[]{:S(2)}) copy-start(bf16[2048,128]{1,0:T(8,128)(2,1)} %wv_h.1) | copy-start | bytes 1572868
  0.6 1.3 %copy-start.3 = (bf16[256,128]{1,0:T(8,128)(2,1)S(1)}, bf16[256,128]{1,0:T(8,128)(2,1)}, u32[]{:S(2)}) copy-start(bf16[256,128]{1,0:T(8,128)(2,1)} %og_ref.1) | copy-start | bytes 196612
  0.7 1.3 %copy-start.4 = (f32[256,1]{0,1:T(1,128)S(1)}, f32[256,1]{0,1:T(1,128)}, u32[]{:S(2)}) copy-start(f32[256,1]{0,1:T(1,128)} %param.10) | copy-start | bytes 3076
  1.9 1.2 %copy-start = (bf16[256,2048]{1,0:T(8,128)(2,1)S(1)}, bf16[256,2048]{1,0:T(8,128)(2,1)}, u32[]{:S(2)}) copy-start(bf16[256,2048]{1,0:T(8,128)(2,1)} %tok_h.1) | copy-start | bytes 3145732
  3.2 1.2 %copy-start.1 = (bf16[2048,256]{1,0:T(8,128)(2,1)S(1)}, bf16[2048,256]{1,0:T(8,128)(2,1)}, u32[]{:S(2)}) copy-start(bf16[2048,256]{1,0:T(8,128)(2,1)} %ww_h.1) | copy-start | bytes 3145732

commit v2 on v1

--- a/solution.py
+++ b/solution.py
@@ -14,7 +14,7 @@
 FEATS = 256
 HALF = 96
 SHARD = 352
-SUB = 176
+SUBS = ((0, 96), (96, 96), (192, 80), (272, 80))
 NEG = -1e30
 
 
@@ -70,14 +70,14 @@
     back = tp_n - 1 - links
 
     def body(
-        tok_h, wf_h, ww_h, wv_h, ld_ref, og_ref,
-        att_ref, ig_ref,
-        tok, wf, ww, wv, insem,
+        tok_h, wf_h, ww_h, wv_h, ld_h, og_h,
+        att_ref, res,
+        tok, wf, ww, wv, ld_ref, og_ref, insem,
         kv, kvs, kvr,
         msg, pm, hb, yb, rb, xb, pb, po,
         cs, cr, ys, yr, xs, xr,
         dkv0, dkv2, dkv4, dsend, prt, m2, m1, r2, r1, gs, gr,
-        part, res, rsb, rss, rsr, ags, agr,
+        part, rsb, rss, rsr, ags, agr,
     ):
         i = lax.axis_index("ctx")
         z = lax.axis_index("tp")
@@ -99,7 +99,9 @@
 
         loads = [
             pltpu.make_async_copy(a, b, insem.at[n])
-            for n, (a, b) in enumerate(((tok_h, tok), (wf_h, wf), (wv_h, wv), (ww_h, ww)))
+            for n, (a, b) in enumerate(
+                ((ld_h, ld_ref), (tok_h, tok), (wf_h, wf), (wv_h, wv), (og_h, og_ref), (ww_h, ww))
+            )
         ]
         for one in loads:
             one.start()
@@ -118,6 +120,7 @@
             copy.start()
             return copy
 
+        loads[0].wait()
         ld = jnp.broadcast_to(ld_ref[...], (DH, ROWS))
         tri = jnp.where(iota((ROWS, ROWS), 1) <= iota((ROWS, ROWS), 0), 1.0, 0.0).astype(F32)
         cum = dot(tri, ld, 1, 1, lax.Precision.HIGHEST)
@@ -137,12 +140,11 @@
         b0 = jnp.where((lane == 136) | ((lane >= 144) & (lane < 160)), 1.0, 0.0)
         wq = jnp.where(lane < 16, 0.5, 1.0)
 
-        for n in range(3):
+        for n in range(1, 4):
             loads[n].wait()
         toks = tok[...]
-        fs = (nn(toks, wf[...]).astype(BF).astype(F32) * 0.5).astype(BF)
+        fs = (nt(toks, wf[...]).astype(BF).astype(F32) * 0.5).astype(BF)
         val = nn(toks, wv[...]).astype(BF)
-        og = og_ref[...]
         ka = nn(fs, ak) + a0
         kb = nn(fs, bk) + b0
         phik = ka * kb * tail1
@@ -175,10 +177,12 @@
                 both = jnp.where(first, jnp.exp(tp_), 1.0) * own
                 both = both + jnp.where(first, 1.0, jnp.exp(to)) * other
                 hb[n] = with_rate(both, to + tp_)
-                state["y"] = [
-                    send(hb.at[n], yb.at[n, k], ys.at[n, k], yr.at[n, k], {"ctx": y_peer(sign * k)})
-                    for k in range(1, ynum)
-                ]
+                far_first = sorted(range(1, ynum), key=lambda k: -min(k, ynum - k))
+                sent = {
+                    k: send(hb.at[n], yb.at[n, k], ys.at[n, k], yr.at[n, k], {"ctx": y_peer(sign * k)})
+                    for k in far_first
+                }
+                state["y"] = [sent[k] for k in range(1, ynum)]
 
             def stage_x():
                 prefix = jnp.zeros((HALF, DH), F32)
@@ -249,10 +253,13 @@
         pl.semaphore_wait(barrier, len(peers))
         fwd[0](tn(phik_b, val), jnp.sum(phik, axis=0, keepdims=True))
 
-        loads[3].wait()
+        loads[4].wait()
+        loads[5].wait()
+        og = og_ref[...]
         win = nn(toks, ww[...]).astype(BF)
         wquery = win[:, :DH]
         kv[4] = jnp.concatenate([win[:, DH:], val], axis=1)
+        fwd[1]()
         hop1 = send(kv.at[4], kv.at[2], kvs.at[0], kvr.at[0], {"ctx": after})
 
         lane32 = iota((1, 32), 1)
@@ -271,7 +278,6 @@
         phiq = qa * qb * wq
         phiq_b = phiq.astype(BF)
 
-        fwd[1]()
         num_in = nn(weights_b, val)
         den_in = jnp.sum(weights, axis=1, keepdims=True)
         hop1.wait()
@@ -371,69 +377,69 @@
 
         for j in range(D // DH):
             cut = slice(j * DH, (j + 1) * DH)
-            term = nt(gwin, ww[cut]) + nt(gval, wv[cut]) + nt(gfeat, wf[cut])
+            term = nt(gwin, ww[cut]) + nt(gval, wv[cut]) + nn(gfeat, wf[:, cut])
             part[j * ROWS : (j + 1) * ROWS] = term.astype(BF)
         tail_rows = tp_n * SHARD - D // DH * ROWS
         part[D // DH * ROWS :] = jnp.zeros((tail_rows, DH), BF)
 
         def rows_of(shard, h):
-            at = lax.rem(shard + 2 * tp_n, tp_n) * SHARD + h * SUB
-            return pl.ds(pl.multiple_of(at, 16), SUB)
-
+            at = lax.rem(shard + 2 * tp_n, tp_n) * SHARD + SUBS[h][0]
+            return pl.ds(pl.multiple_of(at, 16), SUBS[h][1])
+
+        def steps(way, h):
+            return links if way == h % 2 else back
+
+        def slot(way, t, h):
+            return rsb.at[way, t, h, pl.ds(0, SUBS[h][1])]
+
+        sides = ((0, 1, up), (1, -1, down))
         rs = {}
         ag = {}
         for t in range(1, links + 1):
-            for h in range(2):
-                for way in range(2):
-                    if way == 1 and t > back:
+            for h in range(len(SUBS)):
+                for way, sign, peer in sides:
+                    last = steps(way, h)
+                    if t > last:
                         continue
-                    shard = z + links + 1 - t if way == 0 else z - back - 1 + t
-                    if t == 1:
-                        src = part.at[rows_of(shard, h)]
-                    else:
+                    rows = rows_of(z + sign * (last + 1 - t), h)
+                    src = part.at[rows]
+                    if t > 1:
                         rs[way, t - 1, h].wait_recv()
-                        slot = rsb.at[way, t - 1, h]
-                        slot[...] = (
-                            slot[...].astype(F32) + part[rows_of(shard, h)].astype(F32)
-                        ).astype(BF)
-                        src = slot
+                        src = slot(way, t - 1, h)
+                        src[...] = (src[...].astype(F32) + part[rows].astype(F32)).astype(BF)
                     rs[way, t, h] = send(
-                        src, rsb.at[way, t, h], rss.at[way, t, h], rsr.at[way, t, h],
-                        {"tp": up if way == 0 else down},
+                        src, slot(way, t, h), rss.at[way, t, h], rsr.at[way, t, h], {"tp": peer}
                     )
         for t in range(1, links + 1):
-            for h in range(2):
+            for h in range(len(SUBS)):
                 if t == 1:
-                    rs[0, links, h].wait_recv()
-                    rs[1, back, h].wait_recv()
-                    res[rows_of(z, h)] = (
-                        part[rows_of(z, h)].astype(F32)
-                        + rsb[0, links, h].astype(F32)
-                        + rsb[1, back, h].astype(F32)
-                    ).astype(BF)
-                for way in range(2):
-                    if way == 1 and t > back:
+                    rows = rows_of(z, h)
+                    total_in = part[rows].astype(F32)
+                    for way, _, _ in sides:
+                        rs[way, steps(way, h), h].wait_recv()
+                        total_in = total_in + slot(way, steps(way, h), h)[...].astype(F32)
+                    res[rows] = total_in.astype(BF)
+                for way, sign, peer in sides:
+                    if t > steps(way, h):
                         continue
-                    shard = z - t + 1 if way == 0 else z + t - 1
                     if t > 1:
                         ag[way, t - 1, h].wait_recv()
-                    at = rows_of(shard, h)
+                    rows = rows_of(z - sign * (t - 1), h)
                     ag[way, t, h] = send(
-                        res.at[at], res.at[at], ags.at[way, t, h], agr.at[way, t, h],
-                        {"tp": up if way == 0 else down},
+                        res.at[rows], res.at[rows], ags.at[way, t, h], agr.at[way, t, h],
+                        {"tp": peer},
                     )
-        for h in range(2):
-            ag[0, links, h].wait_recv()
-            ag[1, back, h].wait_recv()
+        for h in range(len(SUBS)):
+            for way, _, _ in sides:
+                ag[way, steps(way, h), h].wait_recv()
         for one in list(rs.values()) + list(ag.values()):
             one.wait_send()
-        for j in range(D // DH):
-            ig_ref[:, j * DH : (j + 1) * DH] = res[j * ROWS : (j + 1) * ROWS]
 
     scratch = [
-        pltpu.VMEM((ROWS, D), BF), pltpu.VMEM((D, 32), BF),
+        pltpu.VMEM((ROWS, D), BF), pltpu.VMEM((32, D), BF),
         pltpu.VMEM((D, 2 * DH), BF), pltpu.VMEM((D, DH), BF),
-        pltpu.SemaphoreType.DMA((4,)),
+        pltpu.VMEM((1, ROWS), F32), pltpu.VMEM((ROWS, DH), BF),
+        pltpu.SemaphoreType.DMA((6,)),
         pltpu.VMEM((5, ROWS, 2 * DH), BF),
         pltpu.SemaphoreType.DMA((4,)), pltpu.SemaphoreType.DMA((4,)),
         pltpu.VMEM((2, 2 * HALF, DH), BF), pltpu.VMEM((2, 2 * HALF, DH), BF),
@@ -449,38 +455,67 @@
         pltpu.VMEM((ROWS, 2 * DH), BF), pltpu.VMEM((ROWS, 2 * DH), BF),
         pltpu.VMEM((ROWS, 2 * DH), BF), pltpu.VMEM((ROWS, 2 * DH), BF),
         pltpu.SemaphoreType.DMA((3,)), pltpu.SemaphoreType.DMA((3,)),
-        pltpu.VMEM((tp_n * SHARD, DH), BF), pltpu.VMEM((tp_n * SHARD, DH), BF),
-        pltpu.VMEM((2, links + 1, 2, SUB, DH), BF),
-        pltpu.SemaphoreType.DMA((2, links + 1, 2)), pltpu.SemaphoreType.DMA((2, links + 1, 2)),
-        pltpu.SemaphoreType.DMA((2, links + 1, 2)), pltpu.SemaphoreType.DMA((2, links + 1, 2)),
+        pltpu.VMEM((tp_n * SHARD, DH), BF),
+        pltpu.VMEM((2, links + 1, len(SUBS), SUBS[0][1], DH), BF),
+        pltpu.SemaphoreType.DMA((2, links + 1, len(SUBS))), pltpu.SemaphoreType.DMA((2, links + 1, len(SUBS))),
+        pltpu.SemaphoreType.DMA((2, links + 1, len(SUBS))), pltpu.SemaphoreType.DMA((2, links + 1, len(SUBS))),
     ]
     return body, scratch
+
+
+def write_out(att_ref, res_ref, att_h, ig_h, sem):
+    copies = [
+        pltpu.make_async_copy(
+            res_ref.at[pl.ds(j * ROWS, ROWS)], ig_h.at[:, pl.ds(j * DH, DH)], sem.at[j]
+        )
+        for j in range(D // DH)
+    ]
+    copies.append(pltpu.make_async_copy(att_ref, att_h, sem.at[D // DH]))
+    for one in copies:
+        one.start()
+    for one in copies:
+        one.wait()
 
 
 def solution(mesh):
     ctx_n, tp_n = mesh.shape["ctx"], mesh.shape["tp"]
     body, scratch = kernel_body(ctx_n, tp_n)
+    vmem = pl.BlockSpec(memory_space=pltpu.VMEM)
+    hbm = pl.BlockSpec(memory_space=pltpu.HBM)
 
     def per_device(tokens, feature_weight, window_weight, value_weight, log_decay, out_grad):
-        vmem = pl.BlockSpec(memory_space=pltpu.VMEM)
-        anywhere = pl.BlockSpec(memory_space=pl.ANY)
-        return pl.pallas_call(
+        attended, packed = pl.pallas_call(
             body,
             out_shape=(
                 jax.ShapeDtypeStruct((ROWS, DH), BF),
-                jax.ShapeDtypeStruct((ROWS, D), BF),
+                jax.ShapeDtypeStruct((tp_n * SHARD, DH), BF),
             ),
-            in_specs=[anywhere] * 4 + [vmem, vmem],
+            in_specs=[hbm] * 6,
             out_specs=(vmem, vmem),
             scratch_shapes=scratch,
             compiler_params=pltpu.CompilerParams(
                 collective_id=0, has_side_effects=True, vmem_limit_bytes=48 << 20
             ),
             name="layer",
-        )(
-            tokens, feature_weight, window_weight, value_weight,
-            log_decay.reshape(1, ROWS), out_grad,
-        )
+        )(*(
+            pltpu.with_memory_space_constraint(a, pltpu.HBM)
+            for a in (
+                tokens, feature_weight.T, window_weight, value_weight,
+                log_decay.reshape(1, ROWS), out_grad,
+            )
+        ))
+        return pl.pallas_call(
+            write_out,
+            out_shape=(
+                jax.ShapeDtypeStruct((ROWS, DH), BF),
+                jax.ShapeDtypeStruct((ROWS, D), BF),
+            ),
+            in_specs=[vmem, vmem],
+            out_specs=(hbm, hbm),
+            scratch_shapes=[pltpu.SemaphoreType.DMA((D // DH + 1,))],
+            compiler_params=pltpu.CompilerParams(vmem_limit_bytes=8 << 20),
+            name="write_out",
+        )(attended, packed)
 
     in_specs = (
         P("ctx", None), P(None, "tp"), P(None, "tp"), P(None, "tp"),

time: 102 us -> 98 us (0.961)
  the two profiles are of different devices: /device:TPU:56 before, /device:TPU:54 now
where the time goes in v2:
time: 98 us; the launch traced here: 97.8 us
  Pallas kernels  97.2 us (99%)
    pallas_call x1, Pallas kernels, per_device(): pl.pallas_call(body, out_shape=(jax.ShapeDtypeStruct((ROWS, DH), BF), jax...  96 us

profile of v2, /device:TPU:54, one launch (start us, length us, event | category | flops | bytes accessed | tf_op | source)
XLA Modules:
  0.0 97.8 jit_solution(6412064618451704816)
XLA Ops:
  0.6 96.0 %layer.1 = (bf16[256,128]{1,0:T(8,128)(2,1)S(1)}, bf16[4224,128]{1,0:T(8,128)(2,1)S(1)}) custom-call(bf16[256,2048]{1,0:T(8,128)(2,1)} %tok_h.1, bf16[32,2048]{1,0:T(8,128)(2,1)} %bitcast.2, bf16[2048,256]{1,0:T(8,128)(2,1)} %ww_h.1, bf16[2048,128]{1,0:T(8,128)(2,1)} %wv_h.1, f32[1,256]{1,0:T(1,128)} %bitcast.3, bf16[256,128]{1,0:T(8,128)(2,1)} %og_h.1), custom_call_target="tpu_custom_call" | custom-call | tf_op jit(solution)/shard_map/layer/pallas_call | solution.py:487
  96.7 1.1 %write_out.1 = (bf16[256,128]{1,0:T(8,128)(2,1)}, bf16[256,2048]{1,0:T(8,128)(2,1)}) custom-call(bf16[256,128]{1,0:T(8,128)(2,1)S(1)} %get-tuple-element.4.att_ref, bf16[4224,128]{1,0:T(8,128)(2,1)S(1)} %get-tuple-element.5.res_ref), custom_call_target="tpu_custom_call" | custom-call | tf_op jit(solution)/shard_map/write_out/pallas_call | solution.py:507

commit v3 on v2

--- a/solution.py
+++ b/solution.py
@@ -395,6 +395,7 @@
         sides = ((0, 1, up), (1, -1, down))
         rs = {}
         ag = {}
+        sent_early = set()
         for t in range(1, links + 1):
             for h in range(len(SUBS)):
                 for way, sign, peer in sides:
@@ -410,13 +411,14 @@
                     rs[way, t, h] = send(
                         src, slot(way, t, h), rss.at[way, t, h], rsr.at[way, t, h], {"tp": peer}
                     )
+        finals = {(way, h): rs[way, steps(way, h), h] for way in range(2) for h in range(len(SUBS))}
         for t in range(1, links + 1):
             for h in range(len(SUBS)):
                 if t == 1:
                     rows = rows_of(z, h)
                     total_in = part[rows].astype(F32)
                     for way, _, _ in sides:
-                        rs[way, steps(way, h), h].wait_recv()
+                        finals[way, h].wait_recv()
                         total_in = total_in + slot(way, steps(way, h), h)[...].astype(F32)
                     res[rows] = total_in.astype(BF)
                 for way, sign, peer in sides:
@@ -429,11 +431,20 @@
                         res.at[rows], res.at[rows], ags.at[way, t, h], agr.at[way, t, h],
                         {"tp": peer},
                     )
+                for way in range(2):
+                    done = [rs.pop((way, t, h), None)]
+                    if t > 1:
+                        done.append(ag.get((way, t - 1, h)))
+                        sent_early.add((way, t - 1, h))
+                    for one in done:
+                        if one is not None:
+                            one.wait_send()
         for h in range(len(SUBS)):
             for way, _, _ in sides:
                 ag[way, steps(way, h), h].wait_recv()
-        for one in list(rs.values()) + list(ag.values()):
-            one.wait_send()
+        for key in ag:
+            if key not in sent_early:
+                ag[key].wait_send()
 
     scratch = [
         pltpu.VMEM((ROWS, D), BF), pltpu.VMEM((32, D), BF),

time: 98 us -> 97.9 us (level)
  no operation moved by 1% of the time
where the time goes in v3:
time: 97.9 us; the launch traced here: 97.7 us
  Pallas kernels  97.1 us (99%)
    pallas_call x1, Pallas kernels, per_device(): pl.pallas_call(body, out_shape=(jax.ShapeDtypeStruct((ROWS, DH), BF), jax...  95.9 us

profile of v3, /device:TPU:54, one launch (start us, length us, event | category | flops | bytes accessed | tf_op | source)
XLA Modules:
  0.0 97.7 jit_solution(14808965470435919427)
XLA Ops:
  0.6 95.9 %layer.1 = (bf16[256,128]{1,0:T(8,128)(2,1)S(1)}, bf16[4224,128]{1,0:T(8,128)(2,1)S(1)}) custom-call(bf16[256,2048]{1,0:T(8,128)(2,1)} %tok_h.1, bf16[32,2048]{1,0:T(8,128)(2,1)} %bitcast.2, bf16[2048,256]{1,0:T(8,128)(2,1)} %ww_h.1, bf16[2048,128]{1,0:T(8,128)(2,1)} %wv_h.1, f32[1,256]{1,0:T(1,128)} %bitcast.3, bf16[256,128]{1,0:T(8,128)(2,1)} %og_h.1), custom_call_target="tpu_custom_call" | custom-call | tf_op jit(solution)/shard_map/layer/pallas_call | solution.py:498
  96.6 1.1 %write_out.1 = (bf16[256,128]{1,0:T(8,128)(2,1)}, bf16[256,2048]{1,0:T(8,128)(2,1)}) custom-call(bf16[256,128]{1,0:T(8,128)(2,1)S(1)} %get-tuple-element.4.att_ref, bf16[4224,128]{1,0:T(8,128)(2,1)S(1)} %get-tuple-element.5.res_ref), custom_call_target="tpu_custom_call" | custom-call | tf_op jit(solution)/shard_map/write_out/pallas_call | solution.py:518
